TPU v7x, 256 devices: a whole 4x4x8 slice. The times are simulated.
256 devices in a mesh: sec: 64 (over y, z, core), op: 4 (over x).
Axes of the slice: x: 4, y: 4, z: 8, core: 2. Of those that a mesh axis runs over, the one named last changes fastest.
Arguments:
- wave: bfloat16 [384, 256, 256], P('sec', 'op'), may hold values from -6 to 6
- left_ops: bfloat16 [384, 32, 256, 256], P('sec', 'op'), may hold values from -0.09375 to 0.09375
- right_ops: bfloat16 [384, 32, 256, 256], P('sec', 'op'), may hold values from -0.375 to 0.375
- owner_map: int32 [384, 5], P('sec'), may hold values from 0 to 63, all different within a row; in each aligned block of 6 rows (0 to 5, 6 to 11, ...) at most 2 rows name the same one
- local_map: int32 [384, 5], P('sec'), may hold values from 0 to 5
- op_class: int32 [32], P('op'), may hold values from 0 to 4
Outputs:
- applied: bfloat16 [384, 256, 256], P('sec', 'op')
Inputs may be any that keep to these rules, and one draw needn't show every extreme that they name: `owner_map`: each row names 5 different owners; among the rows of one sec index no owner is named more than 2 times, and that count is reached.
All inputs are finite; a program needn't handle non-finite values.
Results may differ from a plain program's by a relative error of at most 0.0049.
Values may be sent and summed in bfloat16 or wider, within the bound.
A program may use at most 128 MiB of HBM per device.

v0:
```python
import jax
import jax.numpy as jnp
from jax import lax
from jax.sharding import PartitionSpec as P


def shards(wave, left_ops, right_ops, owner_map, local_map, op_class):
    sec_dev, classes = owner_map.shape
    block_size = left_ops.shape[2]
    source = owner_map * sec_dev + local_map
    every_wave = lax.all_gather(wave, "sec", axis=0, tiled=True)
    compact = every_wave[source.reshape(sec_dev * classes)]
    sources = lax.all_gather(compact, "op", axis=1, tiled=True)
    sources = sources.reshape(sec_dev, classes, block_size, block_size)
    chosen = sources[:, op_class]
    lifted = jnp.einsum(
        "tonk,tokm->tonm", left_ops, chosen, preferred_element_type=jnp.float32
    ).astype(jnp.bfloat16)
    partial_value = jnp.einsum(
        "tonm,tokm->tnk", lifted, right_ops, preferred_element_type=jnp.float32
    ).astype(jnp.bfloat16)
    return lax.psum_scatter(partial_value, "op", scatter_dimension=1, tiled=True)


def solution(mesh):
    in_specs = (
        P("sec", "op", None),
        P("sec", "op", None, None),
        P("sec", "op", None, None),
        P("sec", None),
        P("sec", None),
        P("op"),
    )
    out_specs = P("sec", "op", None)
    return jax.shard_map(shards, mesh=mesh, in_specs=in_specs, out_specs=out_specs, check_vma=False)
```

profile of v0, /device:TPU:8, one launch (start us, length us, event | category | flops | bytes accessed | tf_op | source)
XLA Modules:
  0.0 203.4 jit_solution(12440562342349995092)
XLA Ops:
  6.5 0.0 all-gather.4.cloned.1.call-start
  6.5 0.7 all-gather.4.cloned.1.call-update
  7.3 0.0 all-gather.6.cloned.1.call-start
  7.3 0.7 multiply_add_fusion
  8.0 0.1 reshape.34
  8.1 93.7 %all-gather.4.cloned.1.call-done = bf16[384,64,256]{2,1,0:T(8,128)(2,1)} async-done(((bf16[6,64,256]{2,1,0:T(8,128)(2,1)}), bf16[384,64,256]{2,1,0:T(8,128)(2,1)}) %all-gather.4.cloned.1.call-update) | async-done | bytes 12582928 | tf_op jit(solution)/shard_map/all_gather | solution.py:11
  101.8 6.2 %gather_fusion = bf16[30,64,256]{2,1,0:T(8,128)(2,1)} fusion(bf16[384,64,256]{2,1,0:T(8,128)(2,1)} %all-gather.4.cloned.1.call-done, s32[1024]{0:T(1024)S(1)} %pad_clamp_fusion.1), kind=kCustom, calls=%fused_computation | custom fusion | bytes 1966200 | tf_op jit(solution)/shard_map/gather | solution.py:12
  108.0 0.0 all-gather.6.cloned.1.call-update
  108.0 0.0 reduce-scatter.2.cloned.1.call-start
  108.1 0.7 compare_select_fusion
  108.7 46.2 %all-gather.6.cloned.1.call-done = bf16[30,256,256]{2,1,0:T(8,128)(2,1)} async-done(((bf16[30,64,256]{2,1,0:T(8,128)(2,1)}), bf16[30,256,256]{2,1,0:T(8,128)(2,1)}) %all-gather.6.cloned.1.call-update) | async-done | bytes 3932176 | tf_op jit(solution)/shard_map/all_gather | solution.py:13
  154.9 5.7 %gather_fusion.1 = bf16[8,6,256,256]{3,2,1,0:T(8,128)(2,1)} fusion(bf16[6,5,256,256]{3,2,1,0:T(8,128)(2,1)} %bitcast.18, s32[1024]{0:T(1024)S(1)} %pad_clamp_fusion), kind=kCustom, calls=%fused_computation.1 | custom fusion | bytes 12582944 | tf_op jit(solution)/shard_map/gather | solution.py:15
  160.7 10.7 %bitcast_convert_fusion = bf16[6,256,256]{2,1,0:T(8,128)(2,1)} fusion(bf16[6,8,256,256]{3,2,1,0:T(8,128)(2,1)} %param.8, bf16[6,8,256,256]{3,2,1,0:T(8,128)(2,1)} %param.7, bf16[8,6,256,256]{3,2,1,0:T(8,128)(2,1)} %gather_fusion.1), kind=kOutput, calls=%fused_computation.7 | convolution fusion | flops 3224764416 | bytes 19660800 | tf_op jit(solution)/shard_map/tonm,tokm->tnk/dot_general | solution.py:19
  171.4 0.0 reduce-scatter.2.cloned.1.call-update
  171.4 25.4 %reduce-scatter.2.cloned.1.call-done = bf16[6,64,256]{2,1,0:T(8,128)(2,1)} async-done(((bf16[6,256,256]{2,1,0:T(8,128)(2,1)}), bf16[6,64,256]{2,1,0:T(8,128)(2,1)}) %reduce-scatter.2.cloned.1.call-update) | async-done | bytes 196624 | tf_op jit(solution)/shard_map/reduce_scatter | solution.py:22
  (3 shorter events, 0.0 us)
Async XLA Ops:
  6.5 95.2 %all-gather.4.cloned.1.call-start = ((), (), s32[]{:S(2)}) async-start(), calls=%async_computation.1 | async-start | bytes 12779520 | tf_op jit(solution)/shard_map/all_gather | solution.py:11
  7.3 147.7 %all-gather.6.cloned.1.call-start = ((), (), s32[]{:S(2)}) async-start(), calls=%async_computation.3 | async-start | bytes 4915200 | tf_op jit(solution)/shard_map/all_gather | solution.py:13
  108.0 88.8 %reduce-scatter.2.cloned.1.call-start = ((), (), s32[]{:S(2)}) async-start(), calls=%async_computation.2 | async-start | bytes 983040 | tf_op jit(solution)/shard_map/reduce_scatter | solution.py:22
Sparse Core Ops, SparseCore 0:
  10.1 91.6 all-gather.3
  108.1 46.7 all-gather.5
  171.5 25.2 reduce-scatter.1
where the time goes:
time: 204 us; the launch traced here: 203 us
  waiting for transfers between devices  166 us (81%)
  between operations  13.1 us (6%)
  local copies, waits for them, and re-layouts  12 us (6%)
  matrix products  10.7 us (5%)
    all_gather x1, waiting for transfers between devices, shards(): every_wave = lax.all_gather(wave, 'sec', axis=0, tiled=True)  93.7 us
    all_gather x1, waiting for transfers between devices, shards(): sources = lax.all_gather(compact, 'op', axis=1, tiled=True)  46.2 us
    reduce_scatter x1, waiting for transfers between devices, shards(): lax.psum_scatter(partial_value, 'op', scatter_dimension=1, tiled=True)  25.4 us
    dot_general x1, matrix products, shards(): jnp.einsum('tonm,tokm->tnk', lifted, right_ops, preferred_element_type=jn...  10.7 us
    gather x1, local copies, waits for them, and re-layouts, shards(): compact = every_wave[source.reshape(sec_dev * classes)]  6.22 us
    gather x1, local copies, waits for them, and re-layouts, shards(): chosen = sources[:, op_class]  5.72 us
  transfers between devices with their start and end apart: 3, of which 3 were waited for; matrix products, arithmetic and copies ran while one was open for 1% of the time, Pallas kernels for 0%

commit v1 on v0

--- a/solution.py
+++ b/solution.py
@@ -8,7 +8,11 @@
     sec_dev, classes = owner_map.shape
     block_size = left_ops.shape[2]
     source = owner_map * sec_dev + local_map
-    every_wave = lax.all_gather(wave, "sec", axis=0, tiled=True)
+    dev_n = lax.axis_size("sec")
+    block_list = tuple((dev_n if dd == 0 else 1 for dd in range(wave.ndim)))
+    every_wave = lax.all_to_all(
+        jnp.tile(wave, block_list), "sec", split_axis=0, concat_axis=0, tiled=True
+    )
     compact = every_wave[source.reshape(sec_dev * classes)]
     sources = lax.all_gather(compact, "op", axis=1, tiled=True)
     sources = sources.reshape(sec_dev, classes, block_size, block_size)

time: 204 us -> 402 us (1.97)
  waiting for transfers between devices: 166 us -> 346 us
  starting transfers between devices: 0.08 us -> 12.5 us
  local copies, waits for them, and re-layouts: 12 us -> 19 us
    all_to_all x0 -> x1, waiting for transfers between devices: none -> 274 us  [shards(): lax.all_to_all(jnp.tile(wave, block_list), 'sec', split_axis=0, concat_ax...]
    all_gather x1 -> x0, waiting for transfers between devices: 93.7 us -> none  [shards(): every_wave = lax.all_gather(wave, 'sec', axis=0, tiled=True)]
    all_to_all x0 -> x1, starting transfers between devices: none -> 12.4 us  [shards(): lax.all_to_all(jnp.tile(wave, block_list), 'sec', split_axis=0, concat_ax...]
    another operation x0 -> x1, local copies, waits for them, and re-layouts: none -> 7.01 us  [shards(): jnp.tile(wave, block_list)]
  transfers between devices with their start and end apart: 3 -> 3, of which waited for: 3 -> 3; matrix products, arithmetic and copies ran while one was open for 1% -> 0% of each run, Pallas kernels for 0% -> 0%
where the time goes in v1:
time: 402 us
  waiting for transfers between devices  346 us (86%)
  local copies, waits for them, and re-layouts  19 us (5%)
  between operations  13.5 us (3%)
  starting transfers between devices  12.5 us (3%)
  matrix products  10.7 us (3%)
    all_to_all x1, waiting for transfers between devices, shards(): lax.all_to_all(jnp.tile(wave, block_list), 'sec', split_axis=0, concat_ax...  274 us
    all_gather x1, waiting for transfers between devices, shards(): sources = lax.all_gather(compact, 'op', axis=1, tiled=True)  46.5 us
    reduce_scatter x1, waiting for transfers between devices, shards(): lax.psum_scatter(partial_value, 'op', scatter_dimension=1, tiled=True)  25.4 us
    all_to_all x1, starting transfers between devices, shards(): lax.all_to_all(jnp.tile(wave, block_list), 'sec', split_axis=0, concat_ax...  12.4 us
    dot_general x1, matrix products, shards(): jnp.einsum('tonm,tokm->tnk', lifted, right_ops, preferred_element_type=jn...  10.7 us
  transfers between devices with their start and end apart: 3, of which 3 were waited for; matrix products, arithmetic and copies ran while one was open for 0% of the time, Pallas kernels for 0%

profile of v1, /device:TPU:8, one launch (start us, length us, event | category | flops | bytes accessed | tf_op | source)
XLA Modules:
  0.0 402.1 jit_solution(13526671281004678154)
XLA Ops:
  6.5 7.0 %tile.4 = bf16[64,6,64,256]{3,2,1,0:T(8,128)(2,1)} broadcast(bf16[6,64,256]{2,1,0:T(8,128)(2,1)} %param.6), dimensions={1,2,3} | broadcast | bytes 12779520 | tf_op jit(solution)/shard_map/tile | solution.py:14
  13.5 0.0 copy-start
  13.5 0.0 copy-start.1
  13.5 0.0 copy-start.2
  13.6 12.4 %all-to-all-start = ((bf16[384,64,256]{2,1,0:T(8,128)(2,1)}), bf16[384,64,256]{2,1,0:T(8,128)(2,1)}, u32[]{:S(2)}, u32[]{:S(2)}) async-start(bf16[384,64,256]{2,1,0:T(8,128)(2,1)} %bitcast.19), calls=%async_computation | async-start | bytes 25165824 | tf_op jit(solution)/shard_map/all_to_all | solution.py:13
  26.0 0.0 all-gather.3.cloned.1.call-start
  26.0 0.0 copy-done
  26.0 0.0 copy-done.1
  26.0 0.1 reshape.38
  26.1 274.4 %all-to-all-done = bf16[384,64,256]{2,1,0:T(8,128)(2,1)} async-done(((bf16[384,64,256]{2,1,0:T(8,128)(2,1)}), bf16[384,64,256]{2,1,0:T(8,128)(2,1)}, u32[]{:S(2)}, u32[]{:S(2)}) %all-to-all-start) | async-done | bytes 12582944 | tf_op jit(solution)/shard_map/all_to_all | solution.py:13
  300.5 6.2 %gather_fusion = bf16[30,64,256]{2,1,0:T(8,128)(2,1)} fusion(bf16[384,64,256]{2,1,0:T(8,128)(2,1)} %all-to-all-done, s32[1024]{0:T(1024)S(1)} %pad_clamp_fusion.1), kind=kCustom, calls=%fused_computation | custom fusion | bytes 1966200 | tf_op jit(solution)/shard_map/gather | solution.py:16
  306.7 0.0 all-gather.3.cloned.1.call-update
  306.8 0.0 reduce-scatter.2.cloned.1.call-start
  306.8 0.0 copy-done.2
  306.8 46.5 %all-gather.3.cloned.1.call-done = bf16[30,256,256]{2,1,0:T(8,128)(2,1)} async-done(((bf16[30,64,256]{2,1,0:T(8,128)(2,1)}), bf16[30,256,256]{2,1,0:T(8,128)(2,1)}) %all-gather.3.cloned.1.call-update) | async-done | bytes 3932176 | tf_op jit(solution)/shard_map/all_gather | solution.py:17
  353.4 5.7 %gather_fusion.1 = bf16[8,6,256,256]{3,2,1,0:T(8,128)(2,1)} fusion(bf16[6,5,256,256]{3,2,1,0:T(8,128)(2,1)} %bitcast.20, s32[1024]{0:T(1024)S(1)} %pad_clamp_fusion), kind=kCustom, calls=%fused_computation.1 | custom fusion | bytes 12582944 | tf_op jit(solution)/shard_map/gather | solution.py:19
  359.1 10.7 %bitcast_convert_fusion = bf16[6,256,256]{2,1,0:T(8,128)(2,1)} fusion(bf16[6,8,256,256]{3,2,1,0:T(8,128)(2,1)} %param.8, bf16[6,8,256,256]{3,2,1,0:T(8,128)(2,1)} %param.7, bf16[8,6,256,256]{3,2,1,0:T(8,128)(2,1)} %gather_fusion.1), kind=kOutput, calls=%fused_computation.7 | convolution fusion | flops 3224764416 | bytes 19660800 | tf_op jit(solution)/shard_map/tonm,tokm->tnk/dot_general | solution.py:23
  369.8 0.0 reduce-scatter.2.cloned.1.call-update
  369.9 25.4 %reduce-scatter.2.cloned.1.call-done = bf16[6,64,256]{2,1,0:T(8,128)(2,1)} async-done(((bf16[6,256,256]{2,1,0:T(8,128)(2,1)}), bf16[6,64,256]{2,1,0:T(8,128)(2,1)}) %reduce-scatter.2.cloned.1.call-update) | async-done | bytes 196624 | tf_op jit(solution)/shard_map/reduce_scatter | solution.py:26
  (5 shorter events, 0.0 us)
Async XLA Ops:
  13.5 12.5 %copy-start = (s32[6,5]{1,0:T(8,128)S(1)}, s32[6,5]{1,0:T(8,128)}, u32[]{:S(2)}) copy-start(s32[6,5]{1,0:T(8,128)} %param.10) | copy-start | bytes 364
  13.5 12.5 %copy-start.1 = (s32[6,5]{1,0:T(8,128)S(1)}, s32[6,5]{1,0:T(8,128)}, u32[]{:S(2)}) copy-start(s32[6,5]{1,0:T(8,128)} %param.9) | copy-start | bytes 364
  13.5 293.3 %copy-start.2 = (s32[8]{0:T(128)S(1)}, s32[8]{0:T(128)}, u32[]{:S(2)}) copy-start(s32[8]{0:T(128)} %param.11) | copy-start | bytes 100
  13.6 287.0 %all-to-all-start = ((bf16[384,64,256]{2,1,0:T(8,128)(2,1)}), bf16[384,64,256]{2,1,0:T(8,128)(2,1)}, u32[]{:S(2)}, u32[]{:S(2)}) async-start(bf16[384,64,256]{2,1,0:T(8,128)(2,1)} %bitcast.19), calls=%async_computation | async-start | bytes 25165824 | tf_op jit(solution)/shard_map/all_to_all | solution.py:13
  26.0 327.4 %all-gather.3.cloned.1.call-start = ((), (), s32[]{:S(2)}) async-start(), calls=%async_computation.3 | async-start | bytes 4915200 | tf_op jit(solution)/shard_map/all_gather | solution.py:17
  306.8 88.5 %reduce-scatter.2.cloned.1.call-start = ((), (), s32[]{:S(2)}) async-start(), calls=%async_computation.2 | async-start | bytes 983040 | tf_op jit(solution)/shard_map/reduce_scatter | solution.py:26
Sparse Core Ops, SparseCore 0:
  306.9 46.4 all-gather.2
  370.0 25.2 reduce-scatter.1
